TPU v7x, 32 devices: a whole 2x2x4 slice. The times are simulated.
32 devices in a mesh: groups: 2 (over y), tiles: 4 (over z), rhs: 2 (over x), sub: 2 (over core).
Axes of the slice: x: 2, y: 2, z: 4, core: 2. Of those that a mesh axis runs over, the one named last changes fastest.
Arguments:
- sources: bfloat16 [256, 8192], P('rhs', ('groups', 'tiles', 'sub')), parts along dimension 1, may hold values from -6 to 6
- basis_out: bfloat16 [384, 64, 512], P(('groups', 'tiles', 'rhs', 'sub')), parts along dimension 0, may hold values from -0.15625 to 0.15625
- basis_in: bfloat16 [384, 64, 512], P(('groups', 'tiles', 'rhs', 'sub')), parts along dimension 0, may hold values from -0.25 to 0.25
- tile_rank: int32 [384], P(('groups', 'tiles', 'rhs', 'sub')), parts along dimension 0, may hold values from 1 to 64, as said below
- tile_row: int32 [384], P(('groups', 'tiles', 'rhs', 'sub')), parts along dimension 0, may hold values from 0 to 7
- tile_col: int32 [384], P(('groups', 'tiles', 'rhs', 'sub')), parts along dimension 0, may hold values from 0 to 7
- near_blocks: bfloat16 [16, 16, 512, 512], P(('groups', 'tiles', 'sub')), parts along dimension 0, may hold values from -0.0625 to 0.0625
- near_col: int32 [16, 16], P(('groups', 'tiles', 'sub')), parts along dimension 0, may hold values from 0 to 7
- jacobi_inverse: bfloat16 [64, 128, 128], P(('groups', 'tiles', 'sub')), parts along dimension 0
Outputs:
- first_result: bfloat16 [256, 8192], P('rhs', ('groups', 'tiles', 'sub')), parts along dimension 1
- second_result: bfloat16 [256, 8192], P('rhs', ('groups', 'tiles', 'sub')), parts along dimension 1
There are 2 independent parts, one for each index of `groups`. A program takes and returns all parts, laid end to end along the dimension named above; each array names one. Nothing has to cross between parts.
Inputs may be any that keep to these rules, and one draw needn't show every extreme that they name: `tile_rank`: every rank lies in 1 to 64, and some tile has rank 64.
All inputs are finite; a program needn't handle non-finite values.
Results may differ from a plain program's by a relative error of at most 0.03.
Values may be sent and summed in bfloat16 or wider, within the bound.
No kernel may reach another device: no remote copies, remote signals or barrier semaphores. Data moves between devices by JAX's collectives and lax.ppermute only.
A program may use at most 128 MiB of HBM per device.

v0:
```python
import jax
import jax.numpy as jnp
from jax import lax
from jax.sharding import PartitionSpec as P

BLK = 512
RMAX = 64
JB = 128


def tile_terms(running, pieces, gathered):
    basis_out, basis_in, tile_rank, tile_row, tile_col = pieces
    picked = jnp.take(gathered, tile_col, axis=1)
    coefficients = jnp.einsum("ctq,trq->ctr", picked, basis_in, preferred_element_type=jnp.float32)
    rank_iota = lax.broadcasted_iota(jnp.int32, (1, tile_rank.shape[0], RMAX), 2)
    kept_mask = rank_iota < tile_rank[None, :, None]
    coefficients = jnp.where(kept_mask, coefficients, jnp.zeros_like(coefficients)).astype(
        jnp.bfloat16
    )
    contrib = jnp.einsum(
        "ctr,trp->ctp", coefficients, basis_out, preferred_element_type=jnp.float32
    )
    upper = contrib.astype(jnp.bfloat16)
    lower = (contrib - upper.astype(jnp.float32)).astype(jnp.bfloat16)
    block_iota = lax.broadcasted_iota(jnp.int32, (1, running.shape[1]), 1)
    onehot = (tile_row[:, None] == block_iota).astype(jnp.bfloat16)
    placed_upper = jnp.einsum("ctp,tb->cbp", upper, onehot, preferred_element_type=jnp.float32)
    placed_lower = jnp.einsum("ctp,tb->cbp", lower, onehot, preferred_element_type=jnp.float32)
    return placed_upper + placed_lower


def apply_operator(vector, tile_apply, near_blocks, near_col):
    columns = vector.shape[0]
    gathered = lax.all_gather(vector, ("tiles", "sub"), axis=1, tiled=True).reshape(
        columns, -1, BLK
    )
    zero_sums = jnp.zeros(gathered.shape, jnp.float32)
    far_field = tile_apply(zero_sums, gathered).reshape(columns, -1)
    far_field = lax.psum_scatter(
        far_field.astype(jnp.bfloat16), ("tiles", "sub"), scatter_dimension=1, tiled=True
    ).astype(jnp.float32)
    picked = jnp.take(gathered, near_col, axis=1)
    near_field = jnp.einsum(
        "cikq,ikpq->cip", picked, near_blocks, preferred_element_type=jnp.float32
    )
    return (far_field + near_field.reshape(columns, -1)).astype(jnp.bfloat16)


def precondition(field, jacobi_inverse):
    columns = field.shape[0]
    grouped = field.reshape(columns, -1, JB)
    result = jnp.einsum("cgq,gpq->cgp", grouped, jacobi_inverse, preferred_element_type=jnp.float32)
    return result.astype(jnp.bfloat16).reshape(columns, -1)


def local(
    sources,
    basis_out,
    basis_in,
    tile_rank,
    tile_row,
    tile_col,
    near_blocks,
    near_col,
    jacobi_inverse,
):

    def tile_apply(running, gathered):
        return tile_terms(
            running,
            (
                lax.all_gather(basis_out, "rhs", axis=0, tiled=True),
                lax.all_gather(basis_in, "rhs", axis=0, tiled=True),
                lax.all_gather(tile_rank, "rhs", axis=0, tiled=True),
                lax.all_gather(tile_row, "rhs", axis=0, tiled=True),
                lax.all_gather(tile_col, "rhs", axis=0, tiled=True),
            ),
            gathered,
        )

    first_result = precondition(
        apply_operator(sources, tile_apply, near_blocks, near_col), jacobi_inverse
    )
    second_result = precondition(
        apply_operator(first_result, tile_apply, near_blocks, near_col), jacobi_inverse
    )
    return (first_result, second_result)


def solution(mesh):
    return jax.shard_map(
        local,
        mesh=mesh,
        in_specs=(
            P("rhs", ("groups", "tiles", "sub")),
            P(("groups", "tiles", "rhs", "sub"), None, None),
            P(("groups", "tiles", "rhs", "sub"), None, None),
            P(("groups", "tiles", "rhs", "sub")),
            P(("groups", "tiles", "rhs", "sub")),
            P(("groups", "tiles", "rhs", "sub")),
            P(("groups", "tiles", "sub"), None, None, None),
            P(("groups", "tiles", "sub"), None),
            P(("groups", "tiles", "sub"), None, None),
        ),
        out_specs=(P("rhs", ("groups", "tiles", "sub")), P("rhs", ("groups", "tiles", "sub"))),
        check_vma=False,
    )
```

profile of v0, /device:TPU:0, one launch (start us, length us, event | category | flops | bytes accessed | tf_op | source)
XLA Modules:
  0.0 233.3 jit_solution(618950563438700425)
XLA Ops:
  7.2 0.0 copy-start
  7.2 0.0 all-gather.5.cloned.1.call-start
  7.2 1.7 copy.40
  8.9 0.0 all-gather.5.cloned.1.call-update
  8.9 0.0 all-gather.7.cloned.1.call-start
  9.0 0.7 all-gather.7.cloned.1.call-update
  9.7 0.0 all-gather.9.cloned.1.call-start
  9.7 0.7 all-gather.9.cloned.1.call-update
  10.4 0.0 reduce-scatter.3.cloned.1.call-start
  10.5 1.2 dynamic-slice
  12.4 0.9 dynamic-update-slice
  13.2 0.8 dynamic-update-slice.1
  14.1 0.8 dynamic-update-slice.2
  14.9 5.2 %all-reduce.3 = (s32[24]{0:T(128)S(1)}, s32[24]{0:T(128)S(1)}, s32[24]{0:T(128)S(1)}) all-reduce(s32[24]{0:T(128)S(1)} %dynamic-update-slice.2, s32[24]{0:T(128)S(1)} %dynamic-update-slice.1, s32[24]{0:T(128)S(1)} %dynamic-update-slice), channel_id=1, replica_groups=mesh['groups'=2,'tiles'=4,'rhs'=2,'sub'=2] {'rhs'}, use_global_device_ids=true, to_apply=%add.2 | all-reduce | flops 72 | bytes 576
  20.1 0.1 iota_compare_fusion
  20.2 14.8 %all-gather.5.cloned.1.call-done = bf16[128,4096]{0,1:T(8,128)(2,1)} async-done(((bf16[128,512]{0,1:T(8,128)(2,1)}), bf16[128,4096]{0,1:T(8,128)(2,1)}) %all-gather.5.cloned.1.call-update) | async-done | bytes 1048592 | tf_op jit(solution)/shard_map/all_gather | solution.py:34
  35.0 1.5 copy.41
  36.5 2.5 %gather_fusion = bf16[24,128,512]{2,1,0:T(8,128)(2,1)} fusion(bf16[128,8,512]{2,0,1:T(8,128)(2,1)S(1)} %copy.41, s32[1024]{0:T(1024)S(1)} %pad_clamp_fusion.1), kind=kCustom, calls=%fused_computation.clone | custom fusion | bytes 6291552 | tf_op jit(solution)/shard_map/jit(_take)/gather | solution.py:13
  39.0 24.4 %all-gather.7.cloned.1.call-done = bf16[24,64,512]{2,1,0:T(8,128)(2,1)} async-done(((bf16[12,64,512]{2,1,0:T(8,128)(2,1)}), bf16[24,64,512]{2,1,0:T(8,128)(2,1)}) %all-gather.7.cloned.1.call-update) | async-done | bytes 1572880 | tf_op jit(solution)/shard_map/all_gather | solution.py:73
  63.4 28.8 %all-gather.9.cloned.1.call-done = bf16[24,64,512]{2,1,0:T(8,128)(2,1)} async-done(((bf16[12,64,512]{2,1,0:T(8,128)(2,1)}), bf16[24,64,512]{2,1,0:T(8,128)(2,1)}) %all-gather.9.cloned.1.call-update) | async-done | bytes 1572880 | tf_op jit(solution)/shard_map/all_gather | solution.py:72
  92.2 7.7 %fusion.5 = (bf16[128,24,512]{2,0,1:T(8,128)(2,1)}, bf16[128,24,512]{2,0,1:T(8,128)(2,1)}) fusion(bf16[24,64,512]{2,1,0:T(8,128)(2,1)} %all-gather.9.cloned.1.call-done, bf16[24,64,512]{2,1,0:T(8,128)(2,1)} %all-gather.7.cloned.1.call-done, bf16[24,128,512]{2,1,0:T(8,128)(2,1)} %gather_fusion, pred[24]{0:T(512)(128)(4,1)S(1)} %compare_and_fusion, ...), kind=kOutput, calls=%fused_computation.13 | convolution fusion | flops 410910720 | bytes 12584472 | tf_op jit(solution)/shard_map/ctr,trp->ctp/dot_general | solution.py:20
  100.0 0.0 copy-start.2
  100.0 4.3 %fusion.14 = f32[8,128,512]{2,0,1:T(8,128)S(1)} fusion(bf16[128,24,512]{2,0,1:T(8,128)(2,1)} %get-tuple-element.17, s32[24]{0:T(128)S(1)} %get-tuple-element.14), kind=kOutput, calls=%fused_computation.22 | convolution fusion | flops 25166016 | bytes 5242976 | tf_op jit(solution)/shard_map/ctp,tb->cbp/dot_general | solution.py:28
  104.2 0.0 copy-done.2
  104.2 2.3 add_convert_fusion.1
  106.5 0.0 copy-start.4
  106.5 1.4 copy.56
  107.9 0.0 reduce-scatter.3.cloned.1.call-update
  107.9 0.0 all-gather.11.cloned.1.call-start
  108.0 0.0 copy-done.4
  108.0 0.7 gather_fusion.1
  108.7 31.8 %reduce-scatter.3.cloned.1.call-done = bf16[128,512]{1,0:T(8,128)(2,1)} async-done(((bf16[128,4096]{1,0:T(8,128)(2,1)}), bf16[128,512]{1,0:T(8,128)(2,1)}) %reduce-scatter.3.cloned.1.call-update) | async-done | bytes 131088 | tf_op jit(solution)/shard_map/reduce_scatter | solution.py:39
  140.6 6.2 %fusion.93 = bf16[16,4,8,128]{3,2,1,0:T(8,128)(2,1)S(1)} fusion(bf16[1,16,512,512]{3,2,1,0:T(8,128)(2,1)} %param.19, bf16[16,128,512]{2,1,0:T(8,128)(2,1)S(1)} %gather_fusion.1, pred[16]{0:T(512)(128)(4,1)S(1)} %and_bitcast_fusion, bf16[128,512]{1,0:T(8,128)(2,1)} %reduce-scatter.3.cloned.1.call-done), kind=kOutput, calls=%fused_computation.57 | convolution fusion | flops 1074987008 | bytes 10747920 | tf_op jit(solution)/shard_map/cikq,ikpq->cip/dot_general | solution.py:43
  146.8 0.0 copy-done
  146.8 0.9 convolution_convert_fusion.1
  147.7 0.0 all-gather.11.cloned.1.call-update
  147.7 0.2 reduce-scatter.5.cloned.1.call-start
  147.9 20.2 %all-gather.11.cloned.1.call-done = bf16[128,4096]{0,1:T(8,128)(2,1)} async-done(((bf16[128,512]{0,1:T(8,128)(2,1)}), bf16[128,4096]{0,1:T(8,128)(2,1)}) %all-gather.11.cloned.1.call-update) | async-done | bytes 1048592 | tf_op jit(solution)/shard_map/all_gather | solution.py:34
  168.1 3.9 %gather_fusion.2 = bf16[24,128,512]{1,2,0:T(8,128)(2,1)} fusion(bf16[128,8,512]{0,2,1:T(8,128)(2,1)} %bitcast.182, s32[1024]{0:T(1024)S(1)} %pad_clamp_fusion.1), kind=kCustom, calls=%fused_computation.2.clone | custom fusion | bytes 6291552 | tf_op jit(solution)/shard_map/jit(_take)/gather | solution.py:13
  172.0 6.7 %fusion.4 = (bf16[128,24,512]{2,0,1:T(8,128)(2,1)}, bf16[128,24,512]{2,0,1:T(8,128)(2,1)S(1)}) fusion(bf16[24,64,512]{2,1,0:T(8,128)(2,1)} %all-gather.9.cloned.1.call-done, bf16[24,64,512]{2,1,0:T(8,128)(2,1)} %all-gather.7.cloned.1.call-done, bf16[24,128,512]{1,2,0:T(8,128)(2,1)} %gather_fusion.2, pred[24]{0:T(512)(128)(4,1)S(1)} %compare_and_fusion, ...), kind=kOutput, calls=%fused_computation.10 | convolution fusion | flops 410910720 | bytes 12584472 | tf_op jit(solution)/shard_map/ctr,trp->ctp/dot_general | solution.py:20
  178.7 4.1 %fusion.10 = f32[8,128,512]{2,0,1:T(8,128)S(1)} fusion(bf16[128,24,512]{2,0,1:T(8,128)(2,1)} %get-tuple-element.15, s32[24]{0:T(128)S(1)} %get-tuple-element.14), kind=kOutput, calls=%fused_computation.18 | convolution fusion | flops 25166016 | bytes 5242976 | tf_op jit(solution)/shard_map/ctp,tb->cbp/dot_general | solution.py:28
  182.8 2.3 add_convert_fusion
  185.1 0.0 copy-start.3
  185.1 0.0 copy-start.1
  185.2 1.4 copy.57
  186.5 0.0 reduce-scatter.5.cloned.1.call-update
  186.5 0.0 copy-done.3
  186.5 0.8 copy.51
  187.3 0.0 copy-done.1
  187.3 0.5 copy.49
  187.8 2.0 gather_fusion.3
  189.9 28.8 %reduce-scatter.5.cloned.1.call-done = bf16[128,512]{1,0:T(8,128)(2,1)} async-done(((bf16[128,4096]{1,0:T(8,128)(2,1)}), bf16[128,512]{1,0:T(8,128)(2,1)}) %reduce-scatter.5.cloned.1.call-update) | async-done | bytes 131088 | tf_op jit(solution)/shard_map/reduce_scatter | solution.py:39
  218.7 6.8 %fusion.88 = bf16[16,4,8,128]{3,2,1,0:T(8,128)(2,1)S(1)} fusion(bf16[1,16,512,512]{3,2,1,0:T(8,128)(2,1)} %param.19, bf16[16,128,512]{2,1,0:T(8,128)(2,1)} %gather_fusion.3, pred[16]{0:T(512)(128)(4,1)S(1)} %and_bitcast_fusion, bf16[128,512]{1,0:T(8,128)(2,1)} %reduce-scatter.5.cloned.1.call-done), kind=kOutput, calls=%fused_computation.56 | convolution fusion | flops 1074987008 | bytes 10747920 | tf_op jit(solution)/shard_map/cikq,ikpq->cip/dot_general | solution.py:43
  225.5 0.2 convolution_convert_fusion
  225.7 0.8 copy.52
  (9 shorter events, 0.0 us)
Async XLA Ops:
  7.2 139.6 %copy-start = (bf16[4,128,128]{2,1,0:T(8,128)(2,1)S(1)}, bf16[4,128,128]{2,1,0:T(8,128)(2,1)}, u32[]{:S(2)}) copy-start(bf16[4,128,128]{2,1,0:T(8,128)(2,1)} %param.21) | copy-start | bytes 393220
  7.2 27.8 %all-gather.5.cloned.1.call-start = ((), (), s32[]{:S(2)}) async-start(), calls=%async_computation.2 | async-start | bytes 1179648 | tf_op jit(solution)/shard_map/all_gather | solution.py:34
  8.9 54.5 %all-gather.7.cloned.1.call-start = ((), (), s32[]{:S(2)}) async-start(), calls=%async_computation.3 | async-start | bytes 2359296 | tf_op jit(solution)/shard_map/all_gather | solution.py:73
  9.7 82.5 %all-gather.9.cloned.1.call-start = ((), (), s32[]{:S(2)}) async-start(), calls=%async_computation.4 | async-start | bytes 2359296 | tf_op jit(solution)/shard_map/all_gather | solution.py:72
  10.4 130.1 %reduce-scatter.3.cloned.1.call-start = ((), (), s32[]{:S(2)}) async-start(), calls=%async_computation.5 | async-start | bytes 1179648 | tf_op jit(solution)/shard_map/reduce_scatter | solution.py:39
  100.0 4.3 %copy-start.2 = (bf16[128,24,512]{2,0,1:T(8,128)(2,1)S(1)}, bf16[128,24,512]{2,0,1:T(8,128)(2,1)}, u32[]{:S(2)}) copy-start(bf16[128,24,512]{2,0,1:T(8,128)(2,1)} %get-tuple-element.18) | copy-start | bytes 9437188
  106.5 1.5 copy-start.4
  107.9 60.2 %all-gather.11.cloned.1.call-start = ((), (), s32[]{:S(2)}) async-start(), calls=%async_computation.6 | async-start | bytes 1179648 | tf_op jit(solution)/shard_map/all_gather | solution.py:34
  147.7 71.0 %reduce-scatter.5.cloned.1.call-start = ((), (), s32[]{:S(2)}) async-start(), calls=%async_computation.7 | async-start | bytes 1179648 | tf_op jit(solution)/shard_map/reduce_scatter | solution.py:39
  185.1 1.4 copy-start.3
  185.1 2.2 copy-start.1
Sparse Core Ops, SparseCore 0:
  10.2 24.7 all-gather.4
  36.6 26.8 all-gather.6
  65.0 27.1 all-gather.8
  108.0 32.4 reduce-scatter.2
  147.8 20.2 all-gather.10
  186.7 31.9 reduce-scatter.4
where the time goes:
time: 234 us; the launch traced here: 233 us
  waiting for transfers between devices  150 us (64%)
  matrix products  41.5 us (18%)
  local copies, waits for them, and re-layouts  20.9 us (9%)
  between operations  14.9 us (6%)
  blocking collectives  5.19 us (2%)
    reduce_scatter x2, waiting for transfers between devices, apply_operator(): lax.psum_scatter(far_field.astype(jnp.bfloat16), ('tiles', 'sub'), scatte...  60.7 us
    all_gather x2, waiting for transfers between devices, apply_operator(): lax.all_gather(vector, ('tiles', 'sub'), axis=1, tiled=True)  35 us
    all_gather x1, waiting for transfers between devices, tile_apply(): lax.all_gather(basis_out, 'rhs', axis=0, tiled=True)  28.8 us
    all_gather x1, waiting for transfers between devices, tile_apply(): lax.all_gather(basis_in, 'rhs', axis=0, tiled=True)  24.4 us
    dot_general x2, matrix products, tile_terms(): jnp.einsum('ctr,trp->ctp', coefficients, basis_out, preferred_element_typ...  14.4 us
    dot_general x2, matrix products, apply_operator(): jnp.einsum('cikq,ikpq->cip', picked, near_blocks, preferred_element_type=...  13 us
    unnamed x22, local copies, waits for them, and re-layouts  9.77 us
    dot_general x2, matrix products, tile_terms(): jnp.einsum('ctp,tb->cbp', lower, onehot, preferred_element_type=jnp.float32)  8.39 us
  transfers between devices with their start and end apart: 6, of which 6 were waited for; matrix products, arithmetic and copies ran while one was open for 5% of the time, Pallas kernels for 0%

commit v1 on v0

--- a/solution.py
+++ b/solution.py
@@ -6,6 +6,18 @@
 BLK = 512
 RMAX = 64
 JB = 128
+
+
+def gather_by_bits(x, axis, dim):
+    ways, here, step = (lax.axis_size(axis), lax.axis_index(axis), x.shape[dim])
+    line, have = (x, 1)
+    while have < ways:
+        line = jnp.concatenate(
+            [line, lax.ppermute(line, axis, [(d, (d - have) % ways) for d in range(ways)])],
+            axis=dim,
+        )
+        have = 2 * have
+    return jnp.roll(line, here * step, axis=dim)
 
 
 def tile_terms(running, pieces, gathered):
@@ -70,7 +82,7 @@
             running,
             (
                 lax.all_gather(basis_out, "rhs", axis=0, tiled=True),
-                lax.all_gather(basis_in, "rhs", axis=0, tiled=True),
+                gather_by_bits(basis_in, "rhs", 0),
                 lax.all_gather(tile_rank, "rhs", axis=0, tiled=True),
                 lax.all_gather(tile_row, "rhs", axis=0, tiled=True),
                 lax.all_gather(tile_col, "rhs", axis=0, tiled=True),

time: 234 us -> 205 us (0.88)
  waiting for transfers between devices: 150 us -> 107 us
  blocking collectives: 5.19 us -> 13.4 us
  starting transfers between devices: 0.42 us -> 3.39 us
    all_gather x1 -> x0, waiting for transfers between devices: 24.4 us -> none  [tile_apply(): lax.all_gather(basis_in, 'rhs', axis=0, tiled=True)]
    all_gather x2, waiting for transfers between devices: 35 us -> 22.5 us  [apply_operator(): lax.all_gather(vector, ('tiles', 'sub'), axis=1, tiled=True)]
    unnamed x1, blocking collectives: 5.19 us -> 13.4 us
    all_gather x1, waiting for transfers between devices: 28.8 us -> 24.3 us  [tile_apply(): lax.all_gather(basis_out, 'rhs', axis=0, tiled=True)]
    ppermute x0 -> x1, starting transfers between devices: none -> 3 us  [gather_by_bits(): lax.ppermute(line, axis, [(d, (d - have) % ways) for d in range(ways)])]
    unnamed x22 -> x26, local copies, waits for them, and re-layouts: 9.77 us -> 9.75 us
  transfers between devices with their start and end apart: 6 -> 6, of which waited for: 6 -> 5; matrix products, arithmetic and copies ran while one was open for 5% -> 8% of each run, Pallas kernels for 0% -> 0%
where the time goes in v1:
time: 205 us; the launch traced here: 204 us
  waiting for transfers between devices  107 us (52%)
  matrix products  41.7 us (20%)
  local copies, waits for them, and re-layouts  22.3 us (11%)
  between operations  14.6 us (7%)
  blocking collectives  13.4 us (7%)
  starting transfers between devices  3.39 us (2%)
  other arithmetic  2.33 us (1%)
    reduce_scatter x2, waiting for transfers between devices, apply_operator(): lax.psum_scatter(far_field.astype(jnp.bfloat16), ('tiles', 'sub'), scatte...  59.1 us
    all_gather x1, waiting for transfers between devices, tile_apply(): lax.all_gather(basis_out, 'rhs', axis=0, tiled=True)  24.3 us
    all_gather x2, waiting for transfers between devices, apply_operator(): lax.all_gather(vector, ('tiles', 'sub'), axis=1, tiled=True)  22.5 us
    dot_general x2, matrix products, tile_terms(): jnp.einsum('ctr,trp->ctp', coefficients, basis_out, preferred_element_typ...  13.9 us
    dot_general x2, matrix products, apply_operator(): jnp.einsum('cikq,ikpq->cip', picked, near_blocks, preferred_element_type=...  13.6 us
    unnamed x1, blocking collectives  13.4 us
    unnamed x26, local copies, waits for them, and re-layouts  9.75 us
    dot_general x2, matrix products, tile_terms(): jnp.einsum('ctp,tb->cbp', lower, onehot, preferred_element_type=jnp.float32)  8.54 us
  transfers between devices with their start and end apart: 6, of which 5 were waited for; matrix products, arithmetic and copies ran while one was open for 8% of the time, Pallas kernels for 0%

profile of v1, /device:TPU:0, one launch (start us, length us, event | category | flops | bytes accessed | tf_op | source)
XLA Modules:
  0.0 204.4 jit_solution(9321281050885972035)
XLA Ops:
  7.2 0.0 copy-start
  7.2 0.0 all-gather.4.cloned.1.call-start
  7.2 1.7 copy.40
  8.9 0.0 all-gather.4.cloned.1.call-update
  8.9 0.0 all-gather.6.cloned.1.call-start
  9.0 0.7 all-gather.6.cloned.1.call-update
  9.7 0.0 reduce-scatter.3.cloned.1.call-start
  9.7 3.0 %collective-permute-start = (bf16[12,64,512]{2,1,0:T(8,128)(2,1)}, bf16[12,64,512]{2,1,0:T(8,128)(2,1)S(1)}, u32[]{:S(2)}, u32[]{:S(2)}) collective-permute-start(bf16[12,64,512]{2,1,0:T(8,128)(2,1)} %param.17), channel_id=1, source_target_pairs={{0,2},{2,0},{1,3},{3,1},{4,6},{6,4},{5,7},{7,5},{8,10},{10,8},{9,1... | collective-permute-start | bytes 2359304 | tf_op jit(solution)/shard_map/ppermute | solution.py:16
  12.7 1.2 dynamic-slice
  14.6 0.9 dynamic-update-slice
  15.5 0.8 dynamic-update-slice.1
  16.3 0.8 dynamic-update-slice.2
  17.2 13.4 %all-reduce.3 = (s32[24]{0:T(128)S(1)}, s32[24]{0:T(128)S(1)}, s32[24]{0:T(128)S(1)}) all-reduce(s32[24]{0:T(128)S(1)} %dynamic-update-slice.2, s32[24]{0:T(128)S(1)} %dynamic-update-slice.1, s32[24]{0:T(128)S(1)} %dynamic-update-slice), channel_id=1, replica_groups=mesh['groups'=2,'tiles'=4,'rhs'=2,'sub'=2] {'rhs'}, use_global_device_ids=true, to_apply=%add.2 | all-reduce | flops 72 | bytes 576
  30.6 0.1 iota_compare_fusion
  30.7 0.0 collective-permute-done
  30.7 2.2 %fusion.33 = bf16[24,64,512]{2,1,0:T(8,128)(2,1)S(1)} fusion(s32[]{:T(128)S(6)} %select_n.50, bf16[12,64,512]{2,1,0:T(8,128)(2,1)} %param.17, bf16[12,64,512]{2,1,0:T(8,128)(2,1)S(1)} %collective-permute-done), kind=kLoop, calls=%fused_computation.43 | loop fusion | flops 2359296 | bytes 3145732 | tf_op jit(solution)/shard_map/jit(_roll_dynamic)/concatenate | solution.py:20
  32.9 2.1 %all-gather.4.cloned.1.call-done = bf16[128,4096]{0,1:T(8,128)(2,1)} async-done(((bf16[128,512]{0,1:T(8,128)(2,1)}), bf16[128,4096]{0,1:T(8,128)(2,1)}) %all-gather.4.cloned.1.call-update) | async-done | bytes 1048592 | tf_op jit(solution)/shard_map/all_gather | solution.py:46
  35.0 1.5 copy.41
  36.5 2.5 %gather_fusion = bf16[24,128,512]{2,1,0:T(8,128)(2,1)} fusion(bf16[128,8,512]{2,0,1:T(8,128)(2,1)S(1)} %copy.41, s32[1024]{0:T(1024)S(1)} %pad_clamp_fusion.1), kind=kCustom, calls=%fused_computation.clone | custom fusion | bytes 6291552 | tf_op jit(solution)/shard_map/jit(_take)/gather | solution.py:25
  39.0 24.3 %all-gather.6.cloned.1.call-done = bf16[24,64,512]{2,1,0:T(8,128)(2,1)} async-done(((bf16[12,64,512]{2,1,0:T(8,128)(2,1)}), bf16[24,64,512]{2,1,0:T(8,128)(2,1)}) %all-gather.6.cloned.1.call-update) | async-done | bytes 1572880 | tf_op jit(solution)/shard_map/all_gather | solution.py:84
  63.3 7.3 %fusion.5 = (bf16[128,24,512]{2,0,1:T(8,128)(2,1)}, bf16[128,24,512]{2,0,1:T(8,128)(2,1)}) fusion(bf16[24,64,512]{2,1,0:T(8,128)(2,1)} %all-gather.6.cloned.1.call-done, bf16[24,64,512]{2,1,0:T(8,128)(2,1)S(1)} %fusion.33, bf16[24,128,512]{2,1,0:T(8,128)(2,1)} %gather_fusion, pred[24]{0:T(512)(128)(4,1)S(1)} %compare_and_fusion, ...), kind=kOutput, calls=%fused_computation.13 | convolution fusion | flops 410910720 | bytes 12584472 | tf_op jit(solution)/shard_map/ctr,trp->ctp/dot_general | solution.py:32
  70.6 0.0 copy-start.3
  70.6 4.3 %fusion.14 = f32[8,128,512]{2,0,1:T(8,128)S(1)} fusion(bf16[128,24,512]{2,0,1:T(8,128)(2,1)} %get-tuple-element.18, s32[24]{0:T(128)S(1)} %get-tuple-element.15), kind=kOutput, calls=%fused_computation.26 | convolution fusion | flops 25166016 | bytes 5242976 | tf_op jit(solution)/shard_map/ctp,tb->cbp/dot_general | solution.py:40
  74.9 0.0 copy-done.3
  74.9 2.3 %add_convert_fusion.1 = bf16[8,128,512]{2,0,1:T(8,128)(2,1)S(1)} fusion(f32[8,128,512]{2,0,1:T(8,128)S(1)} %fusion.14, bf16[128,24,512]{2,0,1:T(8,128)(2,1)S(1)} %copy-done.3, s32[24]{0:T(128)S(1)} %get-tuple-element.15), kind=kOutput, calls=%fused_computation.39 | convolution fusion | flops 26214592 | bytes 6291552 | tf_op jit(solution)/shard_map/ctp,tb->cbp/dot_general | solution.py:39
  77.2 0.0 copy-start.6
  77.2 1.4 copy.56
  78.5 0.0 reduce-scatter.3.cloned.1.call-update
  78.5 0.0 all-gather.8.cloned.1.call-start
  78.6 0.0 copy-done.6
  78.6 2.0 gather_fusion.1
  80.7 30.3 %reduce-scatter.3.cloned.1.call-done = bf16[128,512]{1,0:T(8,128)(2,1)} async-done(((bf16[128,4096]{1,0:T(8,128)(2,1)}), bf16[128,512]{1,0:T(8,128)(2,1)}) %reduce-scatter.3.cloned.1.call-update) | async-done | bytes 131088 | tf_op jit(solution)/shard_map/reduce_scatter | solution.py:51
  110.9 6.8 %fusion.96 = bf16[16,4,8,128]{3,2,1,0:T(8,128)(2,1)S(1)} fusion(bf16[1,16,512,512]{3,2,1,0:T(8,128)(2,1)} %param.21, bf16[16,128,512]{2,1,0:T(8,128)(2,1)} %gather_fusion.1, pred[16]{0:T(512)(128)(4,1)S(1)} %and_bitcast_fusion, bf16[128,512]{1,0:T(8,128)(2,1)} %reduce-scatter.3.cloned.1.call-done), kind=kOutput, calls=%fused_computation.64 | convolution fusion | flops 1074987008 | bytes 10747920 | tf_op jit(solution)/shard_map/cikq,ikpq->cip/dot_general | solution.py:55
  117.7 0.0 copy-done
  117.8 0.9 convolution_convert_fusion.1
  118.6 0.0 all-gather.8.cloned.1.call-update
  118.6 0.2 reduce-scatter.5.cloned.1.call-start
  118.9 20.4 %all-gather.8.cloned.1.call-done = bf16[128,4096]{0,1:T(8,128)(2,1)} async-done(((bf16[128,512]{0,1:T(8,128)(2,1)}), bf16[128,4096]{0,1:T(8,128)(2,1)}) %all-gather.8.cloned.1.call-update) | async-done | bytes 1048592 | tf_op jit(solution)/shard_map/all_gather | solution.py:46
  139.3 0.0 copy-start.4
  139.3 4.0 %gather_fusion.2 = bf16[24,128,512]{1,2,0:T(8,128)(2,1)} fusion(bf16[128,8,512]{0,2,1:T(8,128)(2,1)} %bitcast.182, s32[1024]{0:T(1024)S(1)} %pad_clamp_fusion.1), kind=kCustom, calls=%fused_computation.2.clone | custom fusion | bytes 6291552 | tf_op jit(solution)/shard_map/jit(_take)/gather | solution.py:25
  143.4 0.0 copy-done.4
  143.4 6.7 %fusion.4 = (bf16[128,24,512]{2,0,1:T(8,128)(2,1)}, bf16[128,24,512]{2,0,1:T(8,128)(2,1)}) fusion(bf16[24,64,512]{2,1,0:T(8,128)(2,1)S(1)} %copy-done.4, bf16[24,64,512]{2,1,0:T(8,128)(2,1)S(1)} %fusion.33, bf16[24,128,512]{1,2,0:T(8,128)(2,1)} %gather_fusion.2, pred[24]{0:T(512)(128)(4,1)S(1)} %compare_and_fusion, pred[24,64]{1,0:T(8,128)(4,1)S(1)} %iota_compare_fusion), kind=kOutput, calls=%fused_computation.10 | convolution fusion | flops 410910720 | bytes 12584472 | tf_op jit(solution)/shard_map/ctr,trp->ctp/dot_general | solution.py:32
  150.0 0.0 copy-start.2
  150.0 4.3 %fusion.10 = f32[8,128,512]{2,0,1:T(8,128)S(1)} fusion(bf16[128,24,512]{2,0,1:T(8,128)(2,1)} %get-tuple-element.16, s32[24]{0:T(128)S(1)} %get-tuple-element.15), kind=kOutput, calls=%fused_computation.22 | convolution fusion | flops 25166016 | bytes 5242976 | tf_op jit(solution)/shard_map/ctp,tb->cbp/dot_general | solution.py:40
  154.3 0.0 copy-done.2
  154.3 2.3 %add_convert_fusion = bf16[8,128,512]{2,0,1:T(8,128)(2,1)S(1)} fusion(f32[8,128,512]{2,0,1:T(8,128)S(1)} %fusion.10, bf16[128,24,512]{2,0,1:T(8,128)(2,1)S(1)} %copy-done.2, s32[24]{0:T(128)S(1)} %get-tuple-element.15), kind=kOutput, calls=%fused_computation.38 | convolution fusion | flops 26214592 | bytes 6291552 | tf_op jit(solution)/shard_map/ctp,tb->cbp/dot_general | solution.py:39
  156.6 0.0 copy-start.5
  156.6 0.0 copy-start.1
  156.6 1.4 copy.57
  158.0 0.0 reduce-scatter.5.cloned.1.call-update
  158.0 0.0 copy-done.5
  158.0 0.8 copy.51
  158.8 0.0 copy-done.1
  158.8 0.5 copy.49
  159.3 2.0 gather_fusion.3
  161.3 28.8 %reduce-scatter.5.cloned.1.call-done = bf16[128,512]{1,0:T(8,128)(2,1)} async-done(((bf16[128,4096]{1,0:T(8,128)(2,1)}), bf16[128,512]{1,0:T(8,128)(2,1)}) %reduce-scatter.5.cloned.1.call-update) | async-done | bytes 131088 | tf_op jit(solution)/shard_map/reduce_scatter | solution.py:51
  190.1 6.8 %fusion.91 = bf16[16,4,8,128]{3,2,1,0:T(8,128)(2,1)S(1)} fusion(bf16[1,16,512,512]{3,2,1,0:T(8,128)(2,1)} %param.21, bf16[16,128,512]{2,1,0:T(8,128)(2,1)} %gather_fusion.3, pred[16]{0:T(512)(128)(4,1)S(1)} %and_bitcast_fusion, bf16[128,512]{1,0:T(8,128)(2,1)} %reduce-scatter.5.cloned.1.call-done), kind=kOutput, calls=%fused_computation.63 | convolution fusion | flops 1074987008 | bytes 10747920 | tf_op jit(solution)/shard_map/cikq,ikpq->cip/dot_general | solution.py:55
  196.9 0.2 convolution_convert_fusion
  197.1 0.8 copy.52
  (9 shorter events, 0.0 us)
Async XLA Ops:
  7.2 110.6 %copy-start = (bf16[4,128,128]{2,1,0:T(8,128)(2,1)S(1)}, bf16[4,128,128]{2,1,0:T(8,128)(2,1)}, u32[]{:S(2)}) copy-start(bf16[4,128,128]{2,1,0:T(8,128)(2,1)} %param.23) | copy-start | bytes 393220
  7.2 27.8 %all-gather.4.cloned.1.call-start = ((), (), s32[]{:S(2)}) async-start(), calls=%async_computation.2 | async-start | bytes 1179648 | tf_op jit(solution)/shard_map/all_gather | solution.py:46
  8.9 54.4 %all-gather.6.cloned.1.call-start = ((), (), s32[]{:S(2)}) async-start(), calls=%async_computation.3 | async-start | bytes 2359296 | tf_op jit(solution)/shard_map/all_gather | solution.py:84
  9.7 101.2 %reduce-scatter.3.cloned.1.call-start = ((), (), s32[]{:S(2)}) async-start(), calls=%async_computation.4 | async-start | bytes 1179648 | tf_op jit(solution)/shard_map/reduce_scatter | solution.py:51
  9.7 21.0 %collective-permute-start = (bf16[12,64,512]{2,1,0:T(8,128)(2,1)}, bf16[12,64,512]{2,1,0:T(8,128)(2,1)S(1)}, u32[]{:S(2)}, u32[]{:S(2)}) collective-permute-start(bf16[12,64,512]{2,1,0:T(8,128)(2,1)} %param.17), channel_id=1, source_target_pairs={{0,2},{2,0},{1,3},{3,1},{4,6},{6,4},{5,7},{7,5},{8,10},{10,8},{9,1... | collective-permute-start | bytes 2359304 | tf_op jit(solution)/shard_map/ppermute | solution.py:16
  70.6 4.3 %copy-start.3 = (bf16[128,24,512]{2,0,1:T(8,128)(2,1)S(1)}, bf16[128,24,512]{2,0,1:T(8,128)(2,1)}, u32[]{:S(2)}) copy-start(bf16[128,24,512]{2,0,1:T(8,128)(2,1)} %get-tuple-element.19) | copy-start | bytes 9437188
  77.2 1.4 copy-start.6
  78.5 60.8 %all-gather.8.cloned.1.call-start = ((), (), s32[]{:S(2)}) async-start(), calls=%async_computation.5 | async-start | bytes 1179648 | tf_op jit(solution)/shard_map/all_gather | solution.py:46
  118.6 71.5 %reduce-scatter.5.cloned.1.call-start = ((), (), s32[]{:S(2)}) async-start(), calls=%async_computation.6 | async-start | bytes 1179648 | tf_op jit(solution)/shard_map/reduce_scatter | solution.py:51
  139.3 4.0 %copy-start.4 = (bf16[24,64,512]{2,1,0:T(8,128)(2,1)S(1)}, bf16[24,64,512]{2,1,0:T(8,128)(2,1)}, u32[]{:S(2)}) copy-start(bf16[24,64,512]{2,1,0:T(8,128)(2,1)} %all-gather.6.cloned.1.call-done) | copy-start | bytes 4718596
  150.0 4.3 %copy-start.2 = (bf16[128,24,512]{2,0,1:T(8,128)(2,1)S(1)}, bf16[128,24,512]{2,0,1:T(8,128)(2,1)}, u32[]{:S(2)}) copy-start(bf16[128,24,512]{2,0,1:T(8,128)(2,1)} %get-tuple-element.17) | copy-start | bytes 9437188
  156.6 1.4 copy-start.5
  156.6 2.2 %copy-start.1 = (bf16[128,4096]{0,1:T(8,128)(2,1)S(1)}, bf16[128,4096]{0,1:T(8,128)(2,1)}, u32[]{:S(2)}) copy-start(bf16[128,4096]{0,1:T(8,128)(2,1)} %all-gather.8.cloned.1.call-done) | copy-start | bytes 3145732
Sparse Core Ops, SparseCore 0:
  10.2 24.7 all-gather.3
  36.6 26.7 all-gather.5
  78.7 32.2 reduce-scatter.2
  118.8 20.5 all-gather.7
  158.1 31.9 reduce-scatter.4
